TPU v7x, 32 devices: a whole 2x2x4 slice. The times are simulated.
32 devices in a mesh: mem: 8 (over y, x, core), reg: 4 (over z).
Axes of the slice: x: 2, y: 2, z: 4, core: 2. Of those that a mesh axis runs over, the one named last changes fastest.
Arguments:
- sample_stack: float32 [64, 11, 8, 256], P('mem', None, 'reg'), may hold values from -6 to 6
- weights: float32 [4, 64], P('reg', 'mem'), may hold values from 0.1 to 10
- offspring: int32 [4, 64], P('reg'), may hold values from 0 to 63
- localize: float32 [8, 256], P('reg'), may hold values from 0.2 to 0.9
Outputs:
- posterior: float32 [64, 11, 8, 256], P('mem', None, 'reg')
Inputs may be any that keep to these rules, and one draw needn't show every extreme that they name: `offspring`: each entry names a member.
All inputs are finite; a program needn't handle non-finite values.
Results may differ from a plain program's by a relative error of at most 0.0021.
Values may be sent and summed in bfloat16 or wider, within the bound.
A program may use at most 64 MiB of HBM per device.

v0:
```python
import jax
import jax.numpy as jnp
from jax import lax
from jax.sharding import PartitionSpec as P

wave_gain = 0.25
advect_gain = 0.1
diffuse_gain = 0.1
small_eps = 1e-05


def extended(block, sides, width):
    for axis, dim in sides:
        count = lax.axis_size(axis)
        forward = [(i, i + 1) for i in range(count - 1)]
        forward.append((count - 1, 0))
        backward = [(target, source) for source, target in forward]
        low = lax.ppermute(
            lax.slice_in_dim(block, block.shape[dim] - width, None, axis=dim), axis, forward
        )
        high = lax.ppermute(lax.slice_in_dim(block, 0, width, axis=dim), axis, backward)
        block = jnp.concatenate([low, block, high], axis=dim)
    return block


def advance(padded):
    centre = padded[:, :, 1:-1]
    upper_rows = padded[:, :, 2:]
    lower_rows = padded[:, :, :-2]
    right_cols = jnp.roll(centre, -1, 3)
    left_cols = jnp.roll(centre, 1, 3)
    slope_east = 0.5 * (right_cols - left_cols)
    slope_north = 0.5 * (upper_rows - lower_rows)
    laplace = right_cols + left_cols + upper_rows + lower_rows - 4.0 * centre
    height = centre[:, 0]
    flow_east = centre[:, 1]
    flow_north = centre[:, 2]
    tracer = centre[:, 3:]
    new_height = height - wave_gain * (slope_east[:, 1] + slope_north[:, 2])
    new_east = flow_east - wave_gain * slope_east[:, 0]
    new_north = flow_north - wave_gain * slope_north[:, 0]
    new_tracer = (
        tracer
        - advect_gain
        * (flow_east[:, None] * slope_east[:, 3:] + flow_north[:, None] * slope_north[:, 3:])
        + diffuse_gain * laplace[:, 3:]
    )
    return jnp.concatenate(
        [new_height[:, None], new_east[:, None], new_north[:, None], new_tracer], axis=1
    )


def single_propagation(model_snapshot):
    padded = extended(model_snapshot, (("reg", 2),), 1)
    return advance(padded)


def per_device(sample_stack, weights, offspring, localize):
    sample_collection = sample_stack.shape[0]
    background_prediction = single_propagation(single_propagation(sample_stack))
    importance_factors = weights[0][:, None, None, None]
    total_local = jnp.sum(weights[0])
    zonal_average_vector = jnp.sum(importance_factors * background_prediction, axis=0)
    weight_total, first_sum = lax.psum((total_local, zonal_average_vector), "mem")
    sample_average_map = first_sum / weight_total
    sample_departure = background_prediction - sample_average_map
    variance = (
        lax.psum(jnp.sum(importance_factors * sample_departure * sample_departure, axis=0), "mem")
        / weight_total
    )
    unrolled_lattice = background_prediction.astype(jnp.bfloat16).reshape(sample_collection, -1)
    source_ids = offspring[0]
    member_base = lax.axis_index("mem") * sample_collection
    own_ids = member_base + jnp.arange(sample_collection, dtype=jnp.int32)
    onehot = (source_ids[:, None] == own_ids[None, :]).astype(jnp.bfloat16)
    sample_duplicates = lax.psum_scatter(
        jnp.dot(onehot, unrolled_lattice, preferred_element_type=jnp.float32).astype(jnp.bfloat16),
        "mem",
        scatter_dimension=0,
        tiled=True,
    ).astype(jnp.float32)
    sample_duplicates = sample_duplicates.reshape(background_prediction.shape)
    cell_weight_value = localize[None, None]
    spread_offset = cell_weight_value * (sample_duplicates - sample_average_map) + (
        1.0 - cell_weight_value
    ) * (background_prediction - sample_average_map)
    total_members = sample_collection * lax.axis_size("mem")
    spread = lax.psum(jnp.sum(spread_offset * spread_offset, axis=0), "mem") / total_members
    scale_ratio = jnp.sqrt((variance + small_eps) / (spread + small_eps))
    return sample_average_map + scale_ratio * spread_offset


def solution(mesh):
    in_specs = (P("mem", None, "reg", None), P("reg", "mem"), P("reg", None), P("reg", None))
    out_specs = P("mem", None, "reg", None)
    return jax.shard_map(
        per_device, mesh=mesh, in_specs=in_specs, out_specs=out_specs, check_vma=False
    )
```

profile of v0, /device:TPU:0, one launch (start us, length us, event | category | flops | bytes accessed | tf_op | source)
XLA Modules:
  0.0 99.8 jit_solution(2924346324299373953)
XLA Ops:
  6.5 1.2 %fusion.51 = (f32[8,11,1,256]{3,2,1,0:T(1,128)S(1)}, f32[8,11,1,256]{3,2,1,0:T(1,128)S(1)}) fusion(f32[8,11,2,256]{3,2,1,0:T(2,128)} %param.4), kind=kLoop, calls=%fused_computation.102 | loop fusion | bytes 360448 | tf_op jit(solution)/shard_map/slice | solution.py:19
  7.8 5.1 %collective-permute-start = (f32[8,11,1,256]{3,2,1,0:T(1,128)S(1)}, f32[8,11,1,256]{3,2,1,0:T(1,128)S(1)}, u32[]{:S(2)}, u32[]{:S(2)}) collective-permute-start(f32[8,11,1,256]{3,2,1,0:T(1,128)S(1)} %get-tuple-element.33), channel_id=1, source_target_pairs={{1,0},{2,1},{3,2},{0,3},{5,4},{6,5},{7,6},{4,7},{9,8},{10,9},{11,1... | collective-permute-start | bytes 270344 | tf_op jit(solution)/shard_map/ppermute | solution.py:21
  12.9 1.1 %fusion.50 = (f32[8,11,2,1]{3,2,1,0:T(2,128)S(1)}, f32[8,11,2,1]{3,2,1,0:T(2,128)S(1)}) fusion(f32[8,11,2,256]{3,2,1,0:T(2,128)} %param.4), kind=kLoop, calls=%fused_computation.101 | loop fusion | bytes 2816 | tf_op jit(solution)/shard_map/jit(_roll_static)/slice | solution.py:30
  14.2 0.4 fusion.3
  14.6 1.1 %collective-permute-done = f32[8,11,1,256]{3,2,1,0:T(1,128)S(1)} collective-permute-done((f32[8,11,1,256]{3,2,1,0:T(1,128)S(1)}, f32[8,11,1,256]{3,2,1,0:T(1,128)S(1)}, u32[]{:S(2)}, u32[]{:S(2)}) %collective-permute-start) | collective-permute-done | bytes 90144 | tf_op jit(solution)/shard_map/ppermute | solution.py:21
  15.7 3.5 %collective-permute-done.1 = f32[8,11,1,256]{3,2,1,0:T(1,128)S(1)} collective-permute-done((f32[8,11,1,256]{3,2,1,0:T(1,128)S(1)}, f32[8,11,1,256]{3,2,1,0:T(1,128)S(1)}, u32[]{:S(2)}, u32[]{:S(2)}) %collective-permute-start.1) | collective-permute-done | bytes 90144 | tf_op jit(solution)/shard_map/ppermute | solution.py:18
  19.2 0.3 fusion.5
  19.6 0.6 fusion.32
  20.6 0.3 fusion.46
  20.9 3.8 %collective-permute-start.2 = (f32[8,11,1,256]{3,2,1,0:T(1,128)S(1)}, f32[8,11,1,256]{3,2,1,0:T(1,128)S(1)}, u32[]{:S(2)}, u32[]{:S(2)}) collective-permute-start(f32[8,11,1,256]{3,2,1,0:T(1,128)S(1)} %get-tuple-element.24), channel_id=1, source_target_pairs={{1,0},{2,1},{3,2},{0,3},{5,4},{6,5},{7,6},{4,7},{9,8},{10,9},{11,1... | collective-permute-start | bytes 270344 | tf_op jit(solution)/shard_map/ppermute | solution.py:21
  24.7 0.4 fusion.1
  25.1 2.1 %collective-permute-done.3 = f32[8,11,1,256]{3,2,1,0:T(1,128)S(1)} collective-permute-done((f32[8,11,1,256]{3,2,1,0:T(1,128)S(1)}, f32[8,11,1,256]{3,2,1,0:T(1,128)S(1)}, u32[]{:S(2)}, u32[]{:S(2)}) %collective-permute-start.3) | collective-permute-done | bytes 90144 | tf_op jit(solution)/shard_map/ppermute | solution.py:18
  27.2 0.4 subtract_multiply_fusion
  27.6 0.4 fusion.25
  28.7 1.2 %convolution_convert_fusion = bf16[64,5632]{1,0:T(8,128)(2,1)} fusion(f32[8,5632]{1,0:T(8,128)S(1)} %concatenate.46, s32[8]{0:T(128)S(1)} %iota_add_fusion, s32[64]{0:T(128)S(1)} %bitcast.21), kind=kOutput, calls=%fused_computation | convolution fusion | flops 6173184 | bytes 901408 | tf_op jit(solution)/shard_map/dot_general | solution.py:77
  30.1 0.6 reduce_sum.39
  30.7 23.4 %all-reduce.1 = (f32[11,2,256]{2,1,0:T(2,128)S(1)}, f32[]{:T(128)}) all-reduce(f32[11,2,256]{2,1,0:T(2,128)S(1)} %get-tuple-element.9, f32[]{:T(128)} %reduce_sum.39), channel_id=1, replica_groups=mesh['mem'=8,'reg'=4] {'mem'}, use_global_device_ids=true, to_apply=%region_1.2 | all-reduce | flops 5633 | bytes 45064 | tf_op jit(solution)/shard_map/psum | solution.py:64
  54.1 0.7 broadcast_divide_fusion
  55.0 11.4 %reduce-scatter.2.cloned.1.call-done = bf16[8,5632]{1,0:T(8,128)(2,1)} async-done(((bf16[64,5632]{1,0:T(8,128)(2,1)}), bf16[8,5632]{1,0:T(8,128)(2,1)}) %reduce-scatter.2.cloned.1.call-update) | async-done | bytes 90128 | tf_op jit(solution)/shard_map/reduce_scatter | solution.py:76
  66.4 0.9 convert
  67.3 1.0 multiply_reduce_fusion
  68.3 23.1 %all-reduce = (f32[11,2,256]{2,1,0:T(2,128)S(1)}, f32[11,2,256]{2,1,0:T(2,128)S(1)}) all-reduce(f32[11,2,256]{2,1,0:T(2,128)S(1)} %reduce_sum.42, f32[11,2,256]{2,1,0:T(2,128)S(1)} %fusion.6), channel_id=1, replica_groups=mesh['mem'=8,'reg'=4] {'mem'}, use_global_device_ids=true, to_apply=%region_8.9 | all-reduce | flops 11264 | bytes 90112 | tf_op jit(solution)/shard_map/psum | solution.py:88
  91.4 0.7 fusion.35
  92.1 0.8 fusion.10
  (30 shorter events, 1.7 us)
Async XLA Ops:
  6.5 7.4 %copy-start = (f32[8,11,2,256]{3,2,1,0:T(2,128)S(1)}, f32[8,11,2,256]{3,2,1,0:T(2,128)}, u32[]{:S(2)}) copy-start(f32[8,11,2,256]{3,2,1,0:T(2,128)} %param.4) | copy-start | bytes 540676
  6.5 59.8 %reduce-scatter.2.cloned.1.call-start = ((), (), s32[]{:S(2)}) async-start(), calls=%async_computation.1 | async-start | bytes 811008 | tf_op jit(solution)/shard_map/reduce_scatter | solution.py:76
  7.8 7.9 %collective-permute-start = (f32[8,11,1,256]{3,2,1,0:T(1,128)S(1)}, f32[8,11,1,256]{3,2,1,0:T(1,128)S(1)}, u32[]{:S(2)}, u32[]{:S(2)}) collective-permute-start(f32[8,11,1,256]{3,2,1,0:T(1,128)S(1)} %get-tuple-element.33), channel_id=1, source_target_pairs={{1,0},{2,1},{3,2},{0,3},{5,4},{6,5},{7,6},{4,7},{9,8},{10,9},{11,1... | collective-permute-start | bytes 270344 | tf_op jit(solution)/shard_map/ppermute | solution.py:21
  12.9 6.3 %collective-permute-start.1 = (f32[8,11,1,256]{3,2,1,0:T(1,128)S(1)}, f32[8,11,1,256]{3,2,1,0:T(1,128)S(1)}, u32[]{:S(2)}, u32[]{:S(2)}) collective-permute-start(f32[8,11,1,256]{3,2,1,0:T(1,128)S(1)} %get-tuple-element.32), channel_id=1, source_target_pairs={{0,1},{1,2},{2,3},{3,0},{4,5},{5,6},{6,7},{7,4},{8,9},{9,10},{10,1... | collective-permute-start | bytes 270344 | tf_op jit(solution)/shard_map/ppermute | solution.py:18
  20.8 6.4 %collective-permute-start.3 = (f32[8,11,1,256]{3,2,1,0:T(1,128)S(1)}, f32[8,11,1,256]{3,2,1,0:T(1,128)S(1)}, u32[]{:S(2)}, u32[]{:S(2)}) collective-permute-start(f32[8,11,1,256]{3,2,1,0:T(1,128)S(1)} %get-tuple-element.25), channel_id=1, source_target_pairs={{0,1},{1,2},{2,3},{3,0},{4,5},{5,6},{6,7},{7,4},{8,9},{9,10},{10,1... | collective-permute-start | bytes 270344 | tf_op jit(solution)/shard_map/ppermute | solution.py:18
  20.9 6.3 %collective-permute-start.2 = (f32[8,11,1,256]{3,2,1,0:T(1,128)S(1)}, f32[8,11,1,256]{3,2,1,0:T(1,128)S(1)}, u32[]{:S(2)}, u32[]{:S(2)}) collective-permute-start(f32[8,11,1,256]{3,2,1,0:T(1,128)S(1)} %get-tuple-element.24), channel_id=1, source_target_pairs={{1,0},{2,1},{3,2},{0,3},{5,4},{6,5},{7,6},{4,7},{9,8},{10,9},{11,1... | collective-permute-start | bytes 270344 | tf_op jit(solution)/shard_map/ppermute | solution.py:21
  27.6 0.7 copy-start.2
  28.1 0.7 copy-start.3
  28.7 1.3 %copy-start.1 = (f32[2,256]{1,0:T(2,128)S(1)}, f32[2,256]{1,0:T(2,128)}, u32[]{:S(2)}) copy-start(f32[2,256]{1,0:T(2,128)} %param.7) | copy-start | bytes 6148
Sparse Core Ops, SparseCore 0:
  30.1 36.2 reduce-scatter.1
where the time goes:
time: 100 us; the launch traced here: 99.8 us
  blocking collectives  46.5 us (46%)
  waiting for transfers between devices  18.1 us (18%)
  between operations  13.6 us (14%)
  starting transfers between devices  8.97 us (9%)
  other arithmetic  7.64 us (8%)
  local copies, waits for them, and re-layouts  3.69 us (4%)
  matrix products  1.24 us (1%)
    psum x1, blocking collectives, per_device(): lax.psum((total_local, zonal_average_vector), 'mem')  23.4 us
    psum x1, blocking collectives, per_device(): lax.psum(jnp.sum(spread_offset * spread_offset, axis=0), 'mem')  23.1 us
    reduce_scatter x1, waiting for transfers between devices, per_device(): lax.psum_scatter(jnp.dot(onehot, unrolled_lattice, preferred_element_type...  11.4 us
    ppermute x2, starting transfers between devices, extended(): lax.ppermute(lax.slice_in_dim(block, 0, width, axis=dim), axis, backward)  8.91 us
    ppermute x2, waiting for transfers between devices, extended(): lax.ppermute(lax.slice_in_dim(block, block.shape[dim] - width, None, axis...  5.62 us
  transfers between devices with their start and end apart: 5, of which 4 were waited for; matrix products, arithmetic and copies ran while one was open for 4% of the time, Pallas kernels for 0%

commit v1 on v0

--- a/solution.py
+++ b/solution.py
@@ -1,12 +1,22 @@
+import functools
 import jax
 import jax.numpy as jnp
 from jax import lax
 from jax.sharding import PartitionSpec as P
+from jax.lax import all_gather
 
 wave_gain = 0.25
 advect_gain = 0.1
 diffuse_gain = 0.1
 small_eps = 1e-05
+
+
+def begin_series_all_on(load, device_axis):
+    before = all_gather(load, axis_name=device_axis).sum(axis=0)
+    return before
+
+
+launch_the_record = functools.partial(begin_series_all_on, device_axis="mem")
 
 
 def extended(block, sides, width):
@@ -85,7 +95,7 @@
         1.0 - cell_weight_value
     ) * (background_prediction - sample_average_map)
     total_members = sample_collection * lax.axis_size("mem")
-    spread = lax.psum(jnp.sum(spread_offset * spread_offset, axis=0), "mem") / total_members
+    spread = launch_the_record(jnp.sum(spread_offset * spread_offset, axis=0)) / total_members
     scale_ratio = jnp.sqrt((variance + small_eps) / (spread + small_eps))
     return sample_average_map + scale_ratio * spread_offset
 

time: 100 us -> 96.5 us (0.965)
  waiting for transfers between devices: 18.1 us -> 6.75 us
  blocking collectives: 46.5 us -> 54.2 us
    reduce_scatter x1, waiting for transfers between devices: 11.4 us -> 0.01 us  [per_device(): lax.psum_scatter(jnp.dot(onehot, unrolled_lattice, preferred_element_type...]
    all_gather x0 -> x1, blocking collectives: none -> 8.31 us  [begin_series_all_on(): before = all_gather(load, axis_name=device_axis).sum(axis=0)]
  transfers between devices with their start and end apart: 5 -> 5, of which waited for: 4 -> 3; matrix products, arithmetic and copies ran while one was open for 4% -> 4% of each run, Pallas kernels for 0% -> 0%
where the time goes in v1:
time: 96.5 us; the launch traced here: 96.1 us
  blocking collectives  54.2 us (56%)
  between operations  13.6 us (14%)
  starting transfers between devices  8.97 us (9%)
  other arithmetic  7.7 us (8%)
  waiting for transfers between devices  6.75 us (7%)
  local copies, waits for them, and re-layouts  3.69 us (4%)
  matrix products  1.24 us (1%)
    psum x1, blocking collectives, per_device(): lax.psum((total_local, zonal_average_vector), 'mem')  23.4 us
    psum x1, blocking collectives, per_device(): lax.psum(jnp.sum(importance_factors * sample_departure * sample_departure...  22.5 us
    ppermute x2, starting transfers between devices, extended(): lax.ppermute(lax.slice_in_dim(block, 0, width, axis=dim), axis, backward)  8.91 us
    all_gather x1, blocking collectives, begin_series_all_on(): before = all_gather(load, axis_name=device_axis).sum(axis=0)  8.31 us
    ppermute x2, waiting for transfers between devices, extended(): lax.ppermute(lax.slice_in_dim(block, block.shape[dim] - width, None, axis...  5.62 us
  transfers between devices with their start and end apart: 5, of which 3 were waited for; matrix products, arithmetic and copies ran while one was open for 4% of the time, Pallas kernels for 0%

profile of v1, /device:TPU:0, one launch (start us, length us, event | category | flops | bytes accessed | tf_op | source)
XLA Modules:
  0.0 96.1 jit_solution(10966484264766346778)
XLA Ops:
  6.5 1.2 %fusion.51 = (f32[8,11,1,256]{3,2,1,0:T(1,128)S(1)}, f32[8,11,1,256]{3,2,1,0:T(1,128)S(1)}) fusion(f32[8,11,2,256]{3,2,1,0:T(2,128)} %param.4), kind=kLoop, calls=%fused_computation.102 | loop fusion | bytes 360448 | tf_op jit(solution)/shard_map/slice | solution.py:29
  7.8 5.1 %collective-permute-start = (f32[8,11,1,256]{3,2,1,0:T(1,128)S(1)}, f32[8,11,1,256]{3,2,1,0:T(1,128)S(1)}, u32[]{:S(2)}, u32[]{:S(2)}) collective-permute-start(f32[8,11,1,256]{3,2,1,0:T(1,128)S(1)} %get-tuple-element.31), channel_id=1, source_target_pairs={{1,0},{2,1},{3,2},{0,3},{5,4},{6,5},{7,6},{4,7},{9,8},{10,9},{11,1... | collective-permute-start | bytes 270344 | tf_op jit(solution)/shard_map/ppermute | solution.py:31
  12.9 1.1 %fusion.50 = (f32[8,11,2,1]{3,2,1,0:T(2,128)S(1)}, f32[8,11,2,1]{3,2,1,0:T(2,128)S(1)}) fusion(f32[8,11,2,256]{3,2,1,0:T(2,128)} %param.4), kind=kLoop, calls=%fused_computation.101 | loop fusion | bytes 2816 | tf_op jit(solution)/shard_map/jit(_roll_static)/slice | solution.py:40
  14.2 0.4 fusion.3
  14.6 1.1 %collective-permute-done = f32[8,11,1,256]{3,2,1,0:T(1,128)S(1)} collective-permute-done((f32[8,11,1,256]{3,2,1,0:T(1,128)S(1)}, f32[8,11,1,256]{3,2,1,0:T(1,128)S(1)}, u32[]{:S(2)}, u32[]{:S(2)}) %collective-permute-start) | collective-permute-done | bytes 90144 | tf_op jit(solution)/shard_map/ppermute | solution.py:31
  15.7 3.5 %collective-permute-done.1 = f32[8,11,1,256]{3,2,1,0:T(1,128)S(1)} collective-permute-done((f32[8,11,1,256]{3,2,1,0:T(1,128)S(1)}, f32[8,11,1,256]{3,2,1,0:T(1,128)S(1)}, u32[]{:S(2)}, u32[]{:S(2)}) %collective-permute-start.1) | collective-permute-done | bytes 90144 | tf_op jit(solution)/shard_map/ppermute | solution.py:28
  19.2 0.3 fusion.5
  19.6 0.6 fusion.32
  20.6 0.3 fusion.46
  20.9 3.8 %collective-permute-start.2 = (f32[8,11,1,256]{3,2,1,0:T(1,128)S(1)}, f32[8,11,1,256]{3,2,1,0:T(1,128)S(1)}, u32[]{:S(2)}, u32[]{:S(2)}) collective-permute-start(f32[8,11,1,256]{3,2,1,0:T(1,128)S(1)} %get-tuple-element.22), channel_id=1, source_target_pairs={{1,0},{2,1},{3,2},{0,3},{5,4},{6,5},{7,6},{4,7},{9,8},{10,9},{11,1... | collective-permute-start | bytes 270344 | tf_op jit(solution)/shard_map/ppermute | solution.py:31
  24.7 0.4 fusion.1
  25.1 2.1 %collective-permute-done.3 = f32[8,11,1,256]{3,2,1,0:T(1,128)S(1)} collective-permute-done((f32[8,11,1,256]{3,2,1,0:T(1,128)S(1)}, f32[8,11,1,256]{3,2,1,0:T(1,128)S(1)}, u32[]{:S(2)}, u32[]{:S(2)}) %collective-permute-start.3) | collective-permute-done | bytes 90144 | tf_op jit(solution)/shard_map/ppermute | solution.py:28
  27.2 0.4 subtract_multiply_fusion
  27.6 0.4 fusion.25
  28.7 1.2 %convolution_convert_fusion = bf16[64,5632]{1,0:T(8,128)(2,1)} fusion(f32[8,5632]{1,0:T(8,128)S(1)} %concatenate.46, s32[8]{0:T(128)S(1)} %iota_add_fusion, s32[64]{0:T(128)S(1)} %bitcast.21), kind=kOutput, calls=%fused_computation | convolution fusion | flops 6173184 | bytes 901408 | tf_op jit(solution)/shard_map/dot_general | solution.py:87
  30.1 0.6 reduce_sum.46
  30.7 23.4 %all-reduce = (f32[11,2,256]{2,1,0:T(2,128)S(1)}, f32[]{:T(128)}) all-reduce(f32[11,2,256]{2,1,0:T(2,128)S(1)} %get-tuple-element.7, f32[]{:T(128)} %reduce_sum.46), channel_id=1, replica_groups=mesh['mem'=8,'reg'=4] {'mem'}, use_global_device_ids=true, to_apply=%region_1.2 | all-reduce | flops 5633 | bytes 45064 | tf_op jit(solution)/shard_map/psum | solution.py:74
  54.1 0.7 broadcast_divide_fusion
  55.0 22.5 %psum.23 = f32[11,2,256]{2,1,0:T(2,128)S(1)} all-reduce(f32[11,2,256]{2,1,0:T(2,128)S(1)} %fusion.6), channel_id=1, replica_groups=mesh['mem'=8,'reg'=4] {'mem'}, use_global_device_ids=true, to_apply=%region_5.6 | all-reduce | flops 5632 | bytes 45056 | tf_op jit(solution)/shard_map/psum | solution.py:78
  77.4 0.9 convert
  78.3 1.0 %multiply_reduce_fusion = f32[5632]{0:T(1024)S(1)} fusion(f32[8,5632]{1,0:T(8,128)S(1)} %concatenate.46, f32[5632]{0:T(1024)S(1)} %mul.204, f32[5632]{0:T(1024)S(1)} %add.97, f32[5632]{0:T(1024)S(1)} %mul.199, bf16[8,5632]{1,0:T(8,128)(2,1)} %reduce-scatter.2.cloned.1.call-done), kind=kLoop, calls=%fused_computation.35 | loop fusion | flops 354816 | bytes 360448 | tf_op jit(solution)/shard_map/reduce_sum | solution.py:98
  79.4 8.3 %all_gather.7 = f32[8,11,2,256]{3,2,1,0:T(2,128)S(1)} all-gather(f32[1,11,2,256]{3,2,1,0:T(2,128)S(1)} %all_gather.6), channel_id=1, replica_groups=mesh['mem'=8,'reg'=4] {'mem'}, dimensions={0}, use_global_device_ids=true | all-gather | bytes 202752 | tf_op jit(solution)/shard_map/all_gather | solution.py:15
  87.7 0.7 fusion.35
  88.4 0.8 fusion.10
  (32 shorter events, 1.8 us)
Async XLA Ops:
  6.5 7.4 %copy-start = (f32[8,11,2,256]{3,2,1,0:T(2,128)S(1)}, f32[8,11,2,256]{3,2,1,0:T(2,128)}, u32[]{:S(2)}) copy-start(f32[8,11,2,256]{3,2,1,0:T(2,128)} %param.4) | copy-start | bytes 540676
  6.5 70.9 %reduce-scatter.2.cloned.1.call-start = ((), (), s32[]{:S(2)}) async-start(), calls=%async_computation.1 | async-start | bytes 811008 | tf_op jit(solution)/shard_map/reduce_scatter | solution.py:86
  7.8 7.9 %collective-permute-start = (f32[8,11,1,256]{3,2,1,0:T(1,128)S(1)}, f32[8,11,1,256]{3,2,1,0:T(1,128)S(1)}, u32[]{:S(2)}, u32[]{:S(2)}) collective-permute-start(f32[8,11,1,256]{3,2,1,0:T(1,128)S(1)} %get-tuple-element.31), channel_id=1, source_target_pairs={{1,0},{2,1},{3,2},{0,3},{5,4},{6,5},{7,6},{4,7},{9,8},{10,9},{11,1... | collective-permute-start | bytes 270344 | tf_op jit(solution)/shard_map/ppermute | solution.py:31
  12.9 6.3 %collective-permute-start.1 = (f32[8,11,1,256]{3,2,1,0:T(1,128)S(1)}, f32[8,11,1,256]{3,2,1,0:T(1,128)S(1)}, u32[]{:S(2)}, u32[]{:S(2)}) collective-permute-start(f32[8,11,1,256]{3,2,1,0:T(1,128)S(1)} %get-tuple-element.30), channel_id=1, source_target_pairs={{0,1},{1,2},{2,3},{3,0},{4,5},{5,6},{6,7},{7,4},{8,9},{9,10},{10,1... | collective-permute-start | bytes 270344 | tf_op jit(solution)/shard_map/ppermute | solution.py:28
  20.8 6.4 %collective-permute-start.3 = (f32[8,11,1,256]{3,2,1,0:T(1,128)S(1)}, f32[8,11,1,256]{3,2,1,0:T(1,128)S(1)}, u32[]{:S(2)}, u32[]{:S(2)}) collective-permute-start(f32[8,11,1,256]{3,2,1,0:T(1,128)S(1)} %get-tuple-element.23), channel_id=1, source_target_pairs={{0,1},{1,2},{2,3},{3,0},{4,5},{5,6},{6,7},{7,4},{8,9},{9,10},{10,1... | collective-permute-start | bytes 270344 | tf_op jit(solution)/shard_map/ppermute | solution.py:28
  20.9 6.3 %collective-permute-start.2 = (f32[8,11,1,256]{3,2,1,0:T(1,128)S(1)}, f32[8,11,1,256]{3,2,1,0:T(1,128)S(1)}, u32[]{:S(2)}, u32[]{:S(2)}) collective-permute-start(f32[8,11,1,256]{3,2,1,0:T(1,128)S(1)} %get-tuple-element.22), channel_id=1, source_target_pairs={{1,0},{2,1},{3,2},{0,3},{5,4},{6,5},{7,6},{4,7},{9,8},{10,9},{11,1... | collective-permute-start | bytes 270344 | tf_op jit(solution)/shard_map/ppermute | solution.py:31
  27.6 0.7 copy-start.2
  28.1 0.7 copy-start.3
  28.7 1.3 %copy-start.1 = (f32[2,256]{1,0:T(2,128)S(1)}, f32[2,256]{1,0:T(2,128)}, u32[]{:S(2)}) copy-start(f32[2,256]{1,0:T(2,128)} %param.7) | copy-start | bytes 6148
Sparse Core Ops, SparseCore 0:
  30.1 36.2 reduce-scatter.1
